TPU v7x, 32 devices: a whole 2x2x4 slice. The times are simulated.
32 devices in a mesh: dp: 8 (over z, y), tensor: 4 (over x, core).
Axes of the slice: x: 2, y: 2, z: 4, core: 2. Of those that a mesh axis runs over, the one named last changes fastest.
Arguments:
- tokens: bfloat16 [2048, 1024], P('dp'), may hold values from -6 to 6
- norm_gain: float32 [1024], replicated, may hold values from 0.25 to 1.75
- w_query: bfloat16 [1024, 1024], P(None, 'tensor'), may hold values from -0.1875 to 0.1875
- w_key: bfloat16 [1024, 1024], P(None, 'tensor'), may hold values from -0.1875 to 0.1875
- w_value: bfloat16 [1024, 2048], P(None, 'tensor'), may hold values from -0.1875 to 0.1875
- w_outgate: bfloat16 [1024, 2048], P(None, 'tensor'), may hold values from -0.1875 to 0.1875
- w_decay: bfloat16 [1024, 8], P(None, 'tensor'), may hold values from -0.1875 to 0.1875
- w_beta: bfloat16 [1024, 8], P(None, 'tensor'), may hold values from -0.1875 to 0.1875
- conv_query: float32 [4, 1024], P(None, 'tensor'), may hold values from -3 to 3
- conv_key: float32 [4, 1024], P(None, 'tensor'), may hold values from -3 to 3
- conv_value: float32 [4, 2048], P(None, 'tensor'), may hold values from -3 to 3
- decay_log: float32 [8], P('tensor'), may hold values from -6 to 0.5
- decay_bias: float32 [8], P('tensor'), may hold values from -1 to 1
- out_norm_gain: float32 [256], replicated, may hold values from 0.25 to 1.75
- w_out: bfloat16 [1024, 2048], P(None, 'tensor'), may hold values from -0.125 to 0.125
- ffn_gain: float32 [1024], replicated, may hold values from 0.25 to 1.75
- w_gate: bfloat16 [1024, 2816], P(None, 'tensor'), may hold values from -0.1875 to 0.1875
- w_up: bfloat16 [1024, 2816], P(None, 'tensor'), may hold values from -0.1875 to 0.1875
- w_down: bfloat16 [1024, 2816], P(None, 'tensor'), may hold values from -0.109375 to 0.109375
- cotangent: bfloat16 [2048, 1024], P('dp'), may hold values from -6 to 6
Outputs:
- layer_out: float32 [2048, 1024], P('dp', 'tensor')
- grad_input: float32 [2048, 1024], P('dp', 'tensor')
- grad_norm_gain: float32 [1024], replicated
- grad_query: float32 [1024, 1024], P('dp', 'tensor')
- grad_key: float32 [1024, 1024], P('dp', 'tensor')
- grad_value: float32 [1024, 2048], P('dp', 'tensor')
- grad_outgate: float32 [1024, 2048], P('dp', 'tensor')
- grad_decay: float32 [1024, 8], P('dp', 'tensor')
- grad_beta: float32 [1024, 8], P('dp', 'tensor')
- grad_conv_query: float32 [4, 1024], P(None, 'tensor')
- grad_conv_key: float32 [4, 1024], P(None, 'tensor')
- grad_conv_value: float32 [4, 2048], P(None, 'tensor')
- grad_decay_log: float32 [8], P('tensor')
- grad_decay_bias: float32 [8], P('tensor')
- grad_out_norm_gain: float32 [256], replicated
- grad_out: float32 [1024, 2048], P('dp', 'tensor')
- grad_ffn_gain: float32 [1024], replicated
- grad_gate: float32 [1024, 2816], P('dp', 'tensor')
- grad_up: float32 [1024, 2816], P('dp', 'tensor')
- grad_down: float32 [1024, 2816], P('dp', 'tensor')
All inputs are finite; a program needn't handle non-finite values.
Results may differ from a plain program's by a relative error of at most 0.012.
Values sent between devices are 32-bit elements; how exact they have to be, the bound alone decides.
No kernel may reach another device: no remote copies, remote signals or barrier semaphores. Data moves between devices by JAX's collectives and lax.ppermute only.
A program may use at most 128 MiB of HBM per device.

v0:
```python
import jax
import jax.numpy as jnp
from jax import lax
from jax.sharding import PartitionSpec as P

GROUP = 64
EPSILON = 1e-06
HIGH = lax.Precision.HIGHEST


def causal_conv(signal, taps):
    length = signal.shape[0]
    count = taps.shape[0]
    padded = jnp.concatenate([jnp.zeros((count - 1, signal.shape[1]), jnp.float32), signal], axis=0)
    total = taps[0] * padded[0:length]
    for index in range(1, count):
        total = total + taps[index] * padded[index : index + length]
    return total


def head_norm(signal, heads):
    shaped = signal.reshape(signal.shape[0], heads, -1)
    return shaped * lax.rsqrt(jnp.sum(shaped * shaped, axis=2, keepdims=True) + EPSILON)


def delta_rule(query, keys, values, beta, logdecay, block):
    length, heads, kdim = keys.shape
    vdim = values.shape[2]
    blocks = length // block
    position = jnp.arange(block)
    lower = (position[:, None] >= position[None, :])[:, :, None]
    strict = (position[:, None] > position[None, :])[:, :, None]
    identity = jnp.eye(block, dtype=jnp.float32)[None]
    squares = block.bit_length() - 2

    def step(state, inputs):
        qblk, kblk, vblk, bblk, gblk = inputs
        cumul = jnp.cumsum(gblk, axis=0)
        ratio = jnp.exp(jnp.where(lower, cumul[:, None, :] - cumul[None, :, :], -1e30))
        growth = jnp.exp(cumul)
        tail = jnp.exp(cumul[-1][None, :] - cumul)
        keykey = jnp.einsum("thd,shd->tsh", kblk, kblk, precision=HIGH)
        strong = jnp.where(strict, keykey * ratio * bblk[:, None, :], 0.0)
        known = jnp.einsum("thd,hed->the", kblk, state, precision=HIGH)
        target = bblk[:, :, None] * (vblk - growth[:, :, None] * known)
        matrix = jnp.transpose(strong, (2, 0, 1))
        inverse = identity - matrix
        power = matrix
        for count in range(squares):
            power = jnp.einsum("hij,hjk->hik", power, power, precision=HIGH)
            inverse = jnp.einsum("hij,hjk->hik", inverse, identity + power, precision=HIGH)
        fresh = jnp.einsum("hts,she->hte", inverse, target, precision=HIGH)
        scores = jnp.where(
            lower, jnp.einsum("thd,shd->tsh", qblk, kblk, precision=HIGH) * ratio, 0.0
        )
        result = growth[:, :, None] * jnp.einsum("thd,hed->the", qblk, state, precision=HIGH)
        result = result + jnp.einsum("tsh,hse->the", scores, fresh, precision=HIGH)
        weighted = tail[:, :, None] * kblk
        new_state = growth[-1][:, None, None] * state + jnp.einsum(
            "hse,shd->hed", fresh, weighted, precision=HIGH
        )
        return (new_state, result)

    start = jnp.zeros((heads, vdim, kdim), jnp.float32)
    inputs = (
        query.reshape(blocks, block, heads, kdim),
        keys.reshape(blocks, block, heads, kdim),
        values.reshape(blocks, block, heads, vdim),
        beta.reshape(blocks, block, heads),
        logdecay.reshape(blocks, block, heads),
    )
    final, results = lax.scan(step, start, inputs)
    return results.reshape(length, heads * vdim)


def mixer(qlin, klin, vlin, alin, blin, conv_q, conv_k, conv_v, rate_log, rate_bias):
    heads = rate_log.shape[0]
    length = qlin.shape[0]
    kdim = qlin.shape[1] // heads
    query = head_norm(jax.nn.silu(causal_conv(qlin, conv_q)), heads) * kdim ** (-0.5)
    keys = head_norm(jax.nn.silu(causal_conv(klin, conv_k)), heads)
    values = jax.nn.silu(causal_conv(vlin, conv_v)).reshape(length, heads, -1)
    beta = jax.nn.sigmoid(blin)
    logdecay = -jnp.exp(rate_log) * jax.nn.softplus(alin + rate_bias)
    return delta_rule(query, keys, values, beta, logdecay, GROUP)


def gated_norm(mixed, zlin, gain):
    length = mixed.shape[0]
    vdim = gain.shape[0]
    shaped = mixed.reshape(length, -1, vdim)
    scale = lax.rsqrt(jnp.mean(shaped * shaped, axis=2, keepdims=True) + EPSILON)
    gates = jax.nn.silu(zlin).reshape(length, -1, vdim)
    return (shaped * scale * gain * gates).reshape(length, -1)


def rms_back(grad_normed, unit, inverse_rms, gain):
    scaled = grad_normed * gain
    return inverse_rms * (scaled - unit * jnp.mean(scaled * unit, axis=1, keepdims=True))


def project(operand, weights):
    return jnp.dot(operand, weights, preferred_element_type=jnp.float32)


def back_dot(operand, weights):
    return jnp.einsum("tc,dc->td", operand, weights, preferred_element_type=jnp.float32)


def outer_sum(operand, other):
    return jnp.einsum("td,tc->dc", operand, other, preferred_element_type=jnp.float32)


def local(
    tokens,
    norm_gain,
    w_query,
    w_key,
    w_value,
    w_outgate,
    w_decay,
    w_beta,
    conv_query,
    conv_key,
    conv_value,
    decay_log,
    decay_bias,
    out_norm_gain,
    w_out,
    ffn_gain,
    w_gate,
    w_up,
    w_down,
    cotangent,
):
    inputs = tokens.astype(jnp.float32)
    inv_first = lax.rsqrt(jnp.mean(inputs * inputs, axis=1, keepdims=True) + EPSILON)
    unit_first = inputs * inv_first
    normed_first = (unit_first * norm_gain).astype(jnp.bfloat16)
    qlin = project(normed_first, w_query)
    klin = project(normed_first, w_key)
    vlin = project(normed_first, w_value)
    zlin = project(normed_first, w_outgate)
    alin = project(normed_first, w_decay)
    blin = project(normed_first, w_beta)
    mixed, mixer_grads_fn = jax.vjp(
        mixer, qlin, klin, vlin, alin, blin, conv_query, conv_key, conv_value, decay_log, decay_bias
    )
    gated, gated_back = jax.vjp(gated_norm, mixed, zlin, out_norm_gain)
    gated_bf = gated.astype(jnp.bfloat16)
    mixer_part = back_dot(gated_bf, w_out)
    resid = inputs + lax.psum(mixer_part, "tensor")
    inv_second = lax.rsqrt(jnp.mean(resid * resid, axis=1, keepdims=True) + EPSILON)
    unit_second = resid * inv_second
    normed_second = (unit_second * ffn_gain).astype(jnp.bfloat16)
    glin = project(normed_second, w_gate)
    ulin = project(normed_second, w_up)
    sigm = jax.nn.sigmoid(glin)
    silu_gate = glin * sigm
    hidden = (silu_gate * ulin).astype(jnp.bfloat16)
    ffn_part = back_dot(hidden, w_down)
    width = resid.shape[1] // lax.axis_size("tensor")
    offset = lax.axis_index("tensor") * width
    ffn_share = lax.psum_scatter(ffn_part, "tensor", scatter_dimension=1, tiled=True)
    layer_out = lax.dynamic_slice_in_dim(resid, offset, width, 1) + ffn_share
    dhidden = project(cotangent, w_down)
    grad_down = outer_sum(cotangent, hidden)
    dglin = (dhidden * ulin * sigm * (1.0 + glin * (1.0 - sigm))).astype(jnp.bfloat16)
    dulin = (dhidden * silu_gate).astype(jnp.bfloat16)
    grad_gate = outer_sum(normed_second, dglin)
    grad_up = outer_sum(normed_second, dulin)
    second_part = back_dot(dglin, w_gate) + back_dot(dulin, w_up)
    dnormed2 = lax.psum(second_part, "tensor")
    grad_ffn_gain = jnp.sum(dnormed2 * unit_second, axis=0)
    dresid = cotangent.astype(jnp.float32) + rms_back(dnormed2, unit_second, inv_second, ffn_gain)
    dresid_bf = dresid.astype(jnp.bfloat16)
    grad_out = outer_sum(dresid_bf, gated_bf)
    dgated = project(dresid_bf, w_out)
    dmixed, dzlin, grad_out_norm = gated_back(dgated)
    dqlin, dklin, dvlin, dalin, dblin, grad_cq, grad_ck, grad_cv, grad_dlog, grad_dbias = (
        mixer_grads_fn(dmixed)
    )
    dq_bf = dqlin.astype(jnp.bfloat16)
    dk_bf = dklin.astype(jnp.bfloat16)
    dv_bf = dvlin.astype(jnp.bfloat16)
    dz_bf = dzlin.astype(jnp.bfloat16)
    da_bf = dalin.astype(jnp.bfloat16)
    db_bf = dblin.astype(jnp.bfloat16)
    grad_query = outer_sum(normed_first, dq_bf)
    grad_key = outer_sum(normed_first, dk_bf)
    grad_value = outer_sum(normed_first, dv_bf)
    grad_outgate = outer_sum(normed_first, dz_bf)
    grad_decay = outer_sum(normed_first, da_bf)
    grad_beta = outer_sum(normed_first, db_bf)
    first_part = (
        back_dot(dq_bf, w_query)
        + back_dot(dk_bf, w_key)
        + back_dot(dv_bf, w_value)
        + back_dot(dz_bf, w_outgate)
        + back_dot(da_bf, w_decay)
        + back_dot(db_bf, w_beta)
    )
    dnormed1, out_norm_total = lax.psum((first_part, grad_out_norm), "tensor")
    grad_norm_gain = jnp.sum(dnormed1 * unit_first, axis=0)
    grad_rows = dresid + rms_back(dnormed1, unit_first, inv_first, norm_gain)
    grad_input = lax.dynamic_slice_in_dim(grad_rows, offset, width, 1)
    sum_norm_gain, sum_ffn_gain, sum_out_norm, sum_dlog, sum_dbias, sum_cq, sum_ck, sum_cv = (
        lax.psum(
            (
                grad_norm_gain,
                grad_ffn_gain,
                out_norm_total,
                grad_dlog,
                grad_dbias,
                grad_cq,
                grad_ck,
                grad_cv,
            ),
            "dp",
        )
    )
    (
        sum_query,
        sum_key,
        sum_value,
        sum_outgate,
        sum_decay,
        sum_beta,
        sum_out,
        sum_gate,
        sum_up,
        sum_down,
    ) = (
        lax.psum_scatter(grad_query, "dp", scatter_dimension=0, tiled=True),
        lax.psum_scatter(grad_key, "dp", scatter_dimension=0, tiled=True),
        lax.psum_scatter(grad_value, "dp", scatter_dimension=0, tiled=True),
        lax.psum_scatter(grad_outgate, "dp", scatter_dimension=0, tiled=True),
        lax.psum_scatter(grad_decay, "dp", scatter_dimension=0, tiled=True),
        lax.psum_scatter(grad_beta, "dp", scatter_dimension=0, tiled=True),
        lax.psum_scatter(grad_out, "dp", scatter_dimension=0, tiled=True),
        lax.psum_scatter(grad_gate, "dp", scatter_dimension=0, tiled=True),
        lax.psum_scatter(grad_up, "dp", scatter_dimension=0, tiled=True),
        lax.psum_scatter(grad_down, "dp", scatter_dimension=0, tiled=True),
    )
    return (
        layer_out,
        grad_input,
        sum_norm_gain,
        sum_query,
        sum_key,
        sum_value,
        sum_outgate,
        sum_decay,
        sum_beta,
        sum_cq,
        sum_ck,
        sum_cv,
        sum_dlog,
        sum_dbias,
        sum_out_norm,
        sum_out,
        sum_ffn_gain,
        sum_gate,
        sum_up,
        sum_down,
    )


def solution(mesh):
    return jax.shard_map(
        local,
        mesh=mesh,
        in_specs=(
            P("dp", None),
            P(),
            P(None, "tensor"),
            P(None, "tensor"),
            P(None, "tensor"),
            P(None, "tensor"),
            P(None, "tensor"),
            P(None, "tensor"),
            P(None, "tensor"),
            P(None, "tensor"),
            P(None, "tensor"),
            P("tensor"),
            P("tensor"),
            P(),
            P(None, "tensor"),
            P(),
            P(None, "tensor"),
            P(None, "tensor"),
            P(None, "tensor"),
            P("dp", None),
        ),
        out_specs=(
            P("dp", "tensor"),
            P("dp", "tensor"),
            P(),
            P("dp", "tensor"),
            P("dp", "tensor"),
            P("dp", "tensor"),
            P("dp", "tensor"),
            P("dp", "tensor"),
            P("dp", "tensor"),
            P(None, "tensor"),
            P(None, "tensor"),
            P(None, "tensor"),
            P("tensor"),
            P("tensor"),
            P(),
            P("dp", "tensor"),
            P(),
            P("dp", "tensor"),
            P("dp", "tensor"),
            P("dp", "tensor"),
        ),
        check_vma=False,
    )
```

profile of v0, /device:TPU:0, one launch (start us, length us, event | category | flops | bytes accessed | tf_op | source)
XLA Modules:
  0.0 1246.9 jit_solution(6733757201012686613)
XLA Ops:
  9.5 1.6 fusion.306
  17.2 1.7 fusion.305
  24.9 95.7 %while.116 = (s32[]{:T(128)}, f32[2,256,128]{2,1,0:T(8,128)S(1)}, f32[4,64,2,256]{3,1,2,0:T(8,128)}, f32[4,64,64,2]{1,2,3,0:T(8,128)}, f32[4,64,2]{1,2,0:T(2,128...) while((s32[]{:T(128)}, f32[2,256,128]{2,1,0:T(8,128)S(1)}, ...), condition=%wide.region_5.6_spmd.clone.clone, body=%wide.region_3.5_spmd.clone.clone.sunk | while | flops 290349312 | bytes 8199534 | solution.py:72
  37.3 1.6 bitcast_dynamic-update-slice_fusion.54
  41.0 1.8 fusion.542
  61.2 1.7 bitcast_dynamic-update-slice_fusion.54
  64.9 1.8 fusion.542
  85.2 1.7 bitcast_dynamic-update-slice_fusion.54
  88.9 1.8 fusion.542
  109.1 1.7 bitcast_dynamic-update-slice_fusion.54
  112.8 1.8 fusion.542
  128.5 38.9 %all-reduce.34.cloned.1.call-done = f32[256,1024]{1,0:T(8,128)} async-done(((f32[256,1024]{1,0:T(8,128)}), f32[256,1024]{1,0:T(8,128)}) %all-reduce.34.cloned.1.call-update) | async-done | bytes 1048592 | tf_op jit(solution)/shard_map/psum | solution.py:152
  169.1 1.5 copy-done.7
  175.6 1.6 convolution_add_fusion.18
  178.1 36.0 %all-reduce.36.cloned.1.call-done = f32[256,1024]{1,0:T(8,128)} async-done(((f32[256,1024]{1,0:T(8,128)}), f32[256,1024]{1,0:T(8,128)}) %all-reduce.36.cloned.1.call-update) | async-done | bytes 1048592 | tf_op jit(solution)/shard_map/psum | solution.py:173
  214.1 2.3 multiply_reduce_fusion
  226.8 213.1 %while.117 = (s32[]{:T(128)}, f32[2,256,128]{2,1,0:T(8,128)S(1)}, f32[4,64,2,128]{3,1,2,0:T(8,128)}, f32[4,64,2,128]{3,1,2,0:T(8,128)}, f32[4,64,2,256]{3,2,1,0:...) while((s32[]{:T(128)}, f32[2,256,128]{2,1,0:T(8,128)S(1)}, ...), condition=%wide.region_24.25_spmd.clone.clone, body=%wide.region_13.24_spmd.clone.clone.sunk | while | flops 580338304 | bytes 14100944 | solution.py:72
  248.5 1.7 fusion.624
  252.7 1.8 fusion.630
  258.8 1.6 fusion.632
  264.4 1.7 reduce_window_sum.46
  277.7 1.5 convolution_add_fusion.34
  301.6 1.7 fusion.624
  305.8 1.8 fusion.630
  311.9 1.6 fusion.632
  317.5 1.7 reduce_window_sum.46
  331.0 1.5 convolution_add_fusion.34
  354.8 1.7 fusion.624
  359.1 1.8 fusion.630
  365.2 1.6 fusion.632
  370.8 1.7 reduce_window_sum.46
  384.2 1.5 convolution_add_fusion.34
  408.1 1.7 fusion.624
  412.4 1.8 fusion.630
  418.5 1.6 fusion.632
  424.0 1.7 reduce_window_sum.46
  437.4 1.5 convolution_add_fusion.34
  441.0 1.9 copy.506
  448.9 1.8 multiply_reduce_fusion.15
  465.2 1.7 fusion.256
  469.4 2.0 convolution_add_fusion.15
  471.5 2.6 fusion.322
  477.2 2.7 fusion.280
  480.0 2.0 fusion.300
  482.9 1.9 fusion.299
  486.0 2.1 fusion.327
  489.1 2.1 fusion.328
  492.3 2.2 convolution_bitcast_fusion.7
  495.2 5.9 psum.93
  501.3 30.1 %reduce-scatter.34.cloned.1.call-done = f32[128,2]{1,0:T(8,128)} async-done(((f32[1024,2]{1,0:T(8,128)}), f32[128,2]{1,0:T(8,128)}) %reduce-scatter.34.cloned.1.call-update) | async-done | bytes 1040
  532.9 63.4 %reduce-scatter.36.cloned.1.call-done = f32[128,2]{1,0:T(8,128)} async-done(((f32[1024,2]{1,0:T(8,128)}), f32[128,2]{1,0:T(8,128)}) %reduce-scatter.36.cloned.1.call-update) | async-done | bytes 1040
  597.8 36.0 %all-reduce.38.cloned.1.call-done = f32[256,1024]{1,0:T(8,128)} async-done(((f32[256,1024]{1,0:T(8,128)}), f32[256,1024]{1,0:T(8,128)}) %all-reduce.38.cloned.1.call-update) | async-done | bytes 1048592 | tf_op jit(solution)/shard_map/psum | solution.py:203
  633.8 2.6 multiply_reduce_fusion.1
  636.4 37.7 %all-reduce.29 = (f32[1024]{0:T(1024)}, f32[4,256]{1,0:T(4,128)}, f32[4,256]{1,0:T(4,128)}, f32[4,512]{1,0:T(4,128)}, f32[2]{0:T(128)}, /*index=5*/f32[2]{0:T(128)}, f32[256]{0:T(256)}, f32[1024]{0:T(1024)}) all-reduce(f32[1024]{0:T(1024)S(1)} %get-tuple-element.2794, ...), channel_id=1, replica_groups=mesh['dp'=8,'tensor'=4] {'dp'}, use_global_device_ids=true, to_apply=%region_30.31 | all-reduce | flops 6404 | bytes 51232 | tf_op jit(solution)/shard_map/psum | solution.py:208
  674.1 1.9 dynamic-slice_add_fusion
  675.9 1.8 dynamic-slice_add_fusion.1
  677.7 52.1 %reduce-scatter.20.cloned.1.call-done = f32[128,256]{1,0:T(8,128)} async-done(((f32[1024,256]{1,0:T(8,128)}), f32[128,256]{1,0:T(8,128)}) %reduce-scatter.20.cloned.1.call-update) | async-done | bytes 131088 | tf_op jit(solution)/shard_map/reduce_scatter | solution.py:235
  729.8 67.4 %reduce-scatter.18.cloned.1.call-done = f32[128,256]{1,0:T(8,128)} async-done(((f32[1024,256]{1,0:T(8,128)}), f32[128,256]{1,0:T(8,128)}) %reduce-scatter.18.cloned.1.call-update) | async-done | bytes 131088 | tf_op jit(solution)/shard_map/reduce_scatter | solution.py:234
  797.1 71.6 %reduce-scatter.26.cloned.1.call-done = f32[128,512]{1,0:T(8,128)} async-done(((f32[1024,512]{1,0:T(8,128)}), f32[128,512]{1,0:T(8,128)}) %reduce-scatter.26.cloned.1.call-update) | async-done | bytes 262160 | tf_op jit(solution)/shard_map/reduce_scatter | solution.py:240
  868.7 71.5 %reduce-scatter.22.cloned.1.call-done = f32[128,512]{1,0:T(8,128)} async-done(((f32[1024,512]{1,0:T(8,128)}), f32[128,512]{1,0:T(8,128)}) %reduce-scatter.22.cloned.1.call-update) | async-done | bytes 262160 | tf_op jit(solution)/shard_map/reduce_scatter | solution.py:236
  940.2 71.9 %reduce-scatter.24.cloned.1.call-done = f32[128,512]{1,0:T(8,128)} async-done(((f32[1024,512]{1,0:T(8,128)}), f32[128,512]{1,0:T(8,128)}) %reduce-scatter.24.cloned.1.call-update) | async-done | bytes 262160 | tf_op jit(solution)/shard_map/reduce_scatter | solution.py:237
  1012.1 75.8 %reduce-scatter.28.cloned.1.call-done = f32[128,704]{0,1:T(8,128)} async-done(((f32[1024,704]{0,1:T(8,128)}), f32[128,704]{0,1:T(8,128)}) %reduce-scatter.28.cloned.1.call-update) | async-done | bytes 360464 | tf_op jit(solution)/shard_map/reduce_scatter | solution.py:241
  1087.9 76.2 %reduce-scatter.30.cloned.1.call-done = f32[128,704]{0,1:T(8,128)} async-done(((f32[1024,704]{0,1:T(8,128)}), f32[128,704]{0,1:T(8,128)}) %reduce-scatter.30.cloned.1.call-update) | async-done | bytes 360464 | tf_op jit(solution)/shard_map/reduce_scatter | solution.py:242
  1164.1 76.2 %reduce-scatter.32.cloned.1.call-done = f32[128,704]{0,1:T(8,128)} async-done(((f32[1024,704]{0,1:T(8,128)}), f32[128,704]{0,1:T(8,128)}) %reduce-scatter.32.cloned.1.call-update) | async-done | bytes 360464 | tf_op jit(solution)/shard_map/reduce_scatter | solution.py:243
  (964 shorter events, 333.3 us)
Async XLA Ops:
  7.2 165.6 %copy-start = (bf16[1024,704]{0,1:T(8,128)(2,1)S(1)}, bf16[1024,704]{0,1:T(8,128)(2,1)}, u32[]{:S(2)}) copy-start(bf16[1024,704]{0,1:T(8,128)(2,1)} %param.42) | copy-start | bytes 4325380
  7.2 160.2 %all-reduce.34.cloned.1.call-start = ((), (), s32[]{:S(2)}) async-start(), calls=%async_computation.11 | async-start | bytes 2097152 | tf_op jit(solution)/shard_map/psum | solution.py:152
  8.6 14.5 %copy-start.77 = (f32[256]{0:T(256)}, f32[256]{0:T(256)S(1)}, u32[]{:S(2)}) copy-start(f32[256]{0:T(256)S(1)} %add_rsqrt_fusion.3) | copy-start | bytes 3076
  14.8 8.7 copy-start.64
  14.8 8.8 copy-start.62
  24.9 7.9 copy-start.81
  24.9 7.9 copy-start.83
  25.4 8.4 copy-start.37
  25.4 10.7 copy-start.26
  40.9 7.8 copy-start.82
  40.9 7.8 copy-start.84
  48.8 8.0 copy-start.81
  48.8 8.0 copy-start.83
  49.3 8.4 copy-start.37
  49.3 10.7 copy-start.26
  64.9 7.9 copy-start.82
  64.9 7.9 copy-start.84
  72.8 7.9 copy-start.81
  72.8 7.9 copy-start.83
  73.3 8.3 copy-start.37
  73.4 10.7 copy-start.26
  88.9 7.8 copy-start.82
  88.9 7.8 copy-start.84
  96.7 8.0 copy-start.81
  96.7 8.0 copy-start.83
  97.2 8.3 copy-start.37
  97.2 10.7 copy-start.26
  112.8 7.8 copy-start.82
  112.8 7.8 copy-start.84
  128.3 40.7 %copy-start.80 = (f32[1024]{0:T(1024)S(1)}, f32[1024]{0:T(1024)}, u32[]{:S(2)}) copy-start(f32[1024]{0:T(1024)} %param.39) | copy-start | bytes 12292
  128.3 85.8 %all-reduce.36.cloned.1.call-start = ((), (), s32[]{:S(2)}) async-start(), calls=%async_computation.13 | async-start | bytes 2097152 | tf_op jit(solution)/shard_map/psum | solution.py:173
  168.9 47.6 %copy-start.2 = (f32[256,1024]{1,0:T(8,128)}, f32[256,1024]{1,0:T(8,128)S(1)}, u32[]{:S(2)}) copy-start(f32[256,1024]{1,0:T(8,128)S(1)} %get-tuple-element.3009) | copy-start | bytes 3145732
  177.2 354.2 %reduce-scatter.34.cloned.1.call-start = ((), (), s32[]{:S(2)}) async-start(), calls=%async_computation.23 | async-start | bytes 589824
  228.1 9.0 copy-start.29
  234.3 9.8 copy-start.28
  234.9 9.7 copy-start.65
  271.1 8.2 copy-start.68
  280.0 7.6 copy-start.30
  281.3 9.0 copy-start.29
  287.5 9.8 copy-start.28
  288.1 9.7 copy-start.65
  324.2 8.3 copy-start.68
  333.2 7.6 copy-start.30
  334.5 9.0 copy-start.29
  340.7 9.8 copy-start.28
  341.3 9.7 copy-start.65
  377.5 8.3 copy-start.68
  387.8 9.0 copy-start.29
  394.0 9.8 copy-start.28
  394.6 9.7 copy-start.65
  430.8 8.2 copy-start.68
  468.1 128.2 %reduce-scatter.36.cloned.1.call-start = ((), (), s32[]{:S(2)}) async-start(), calls=%async_computation.24 | async-start | bytes 589824
  469.4 164.4 %all-reduce.38.cloned.1.call-start = ((), (), s32[]{:S(2)}) async-start(), calls=%async_computation.14 | async-start | bytes 2097152 | tf_op jit(solution)/shard_map/psum | solution.py:203
  471.5 204.4 %reduce-scatter.16.cloned.1.call-start = ((), (), s32[]{:S(2)}) async-start(), calls=%async_computation.12 | async-start | bytes 1310720 | tf_op jit(solution)/shard_map/reduce_scatter | solution.py:164
  474.1 255.6 %reduce-scatter.20.cloned.1.call-start = ((), (), s32[]{:S(2)}) async-start(), calls=%async_computation.16 | async-start | bytes 1179648 | tf_op jit(solution)/shard_map/reduce_scatter | solution.py:235
  475.7 321.5 %reduce-scatter.18.cloned.1.call-start = ((), (), s32[]{:S(2)}) async-start(), calls=%async_computation.15 | async-start | bytes 1179648 | tf_op jit(solution)/shard_map/reduce_scatter | solution.py:234
  477.2 391.5 %reduce-scatter.26.cloned.1.call-start = ((), (), s32[]{:S(2)}) async-start(), calls=%async_computation.19 | async-start | bytes 2359296 | tf_op jit(solution)/shard_map/reduce_scatter | solution.py:240
  480.0 460.2 %reduce-scatter.22.cloned.1.call-start = ((), (), s32[]{:S(2)}) async-start(), calls=%async_computation.17 | async-start | bytes 2359296 | tf_op jit(solution)/shard_map/reduce_scatter | solution.py:236
  482.0 530.1 %reduce-scatter.24.cloned.1.call-start = ((), (), s32[]{:S(2)}) async-start(), calls=%async_computation.18 | async-start | bytes 2359296 | tf_op jit(solution)/shard_map/reduce_scatter | solution.py:237
  484.9 603.1 %reduce-scatter.28.cloned.1.call-start = ((), (), s32[]{:S(2)}) async-start(), calls=%async_computation.20 | async-start | bytes 3244032 | tf_op jit(solution)/shard_map/reduce_scatter | solution.py:241
  488.1 676.0 %reduce-scatter.30.cloned.1.call-start = ((), (), s32[]{:S(2)}) async-start(), calls=%async_computation.21 | async-start | bytes 3244032 | tf_op jit(solution)/shard_map/reduce_scatter | solution.py:242
  491.2 749.2 %reduce-scatter.32.cloned.1.call-start = ((), (), s32[]{:S(2)}) async-start(), calls=%async_computation.22 | async-start | bytes 3244032 | tf_op jit(solution)/shard_map/reduce_scatter | solution.py:243
  597.8 38.6 %copy-start.101 = (f32[1024]{0:T(1024)S(1)}, f32[1024]{0:T(1024)}, u32[]{:S(2)}) copy-start(f32[1024]{0:T(1024)} %get-tuple-element.2786) | copy-start | bytes 12292
  597.8 38.6 %copy-start.141 = (f32[2]{0:T(128)S(1)}, f32[2]{0:T(128)}, u32[]{:S(2)}) copy-start(f32[2]{0:T(128)} %get-tuple-element.2998) | copy-start | bytes 28
  (161 other events, 470.2 us)
Sparse Core Ops, SparseCore 0:
  128.4 39.0 all-reduce.33
  177.4 36.7 all-reduce.35
  468.2 63.1 reduce-scatter.33
  534.6 61.6 reduce-scatter.35
  598.5 35.2 all-reduce.37
  636.2 25.2 reduce-scatter.15
  665.5 64.2 reduce-scatter.19
  733.7 63.3 reduce-scatter.17
  801.2 67.4 reduce-scatter.25
  872.6 67.4 reduce-scatter.21
  944.3 67.7 reduce-scatter.23
  1016.1 71.8 reduce-scatter.27
  1092.1 72.0 reduce-scatter.29
  1168.1 72.1 reduce-scatter.31
where the time goes:
time: 1250 us
  waiting for transfers between devices  767 us (61%)
  matrix products  230 us (18%)
  local copies, waits for them, and re-layouts  107 us (9%)
  other arithmetic  80.2 us (6%)
  blocking collectives  43.6 us (3%)
  between operations  15.7 us (1%)
    unnamed x16, waiting for transfers between devices  93.8 us
    reduce_scatter x1, waiting for transfers between devices, local(): lax.psum_scatter(grad_down, 'dp', scatter_dimension=0, tiled=True)  76.2 us
    reduce_scatter x1, waiting for transfers between devices, local(): lax.psum_scatter(grad_up, 'dp', scatter_dimension=0, tiled=True)  76.2 us
    reduce_scatter x1, waiting for transfers between devices, local(): lax.psum_scatter(grad_gate, 'dp', scatter_dimension=0, tiled=True)  75.8 us
    reduce_scatter x1, waiting for transfers between devices, local(): lax.psum_scatter(grad_outgate, 'dp', scatter_dimension=0, tiled=True)  71.9 us
    reduce_scatter x1, waiting for transfers between devices, local(): lax.psum_scatter(grad_out, 'dp', scatter_dimension=0, tiled=True)  71.6 us
    reduce_scatter x1, waiting for transfers between devices, local(): lax.psum_scatter(grad_value, 'dp', scatter_dimension=0, tiled=True)  71.5 us
    reduce_scatter x1, waiting for transfers between devices, local(): lax.psum_scatter(grad_query, 'dp', scatter_dimension=0, tiled=True)  67.4 us
  transfers between devices with their start and end apart: 14, of which 13 were waited for; matrix products, arithmetic and copies ran while one was open for 3% of the time, Pallas kernels for 0%

commit v1 on v0

--- a/solution.py
+++ b/solution.py
@@ -170,7 +170,7 @@
     grad_gate = outer_sum(normed_second, dglin)
     grad_up = outer_sum(normed_second, dulin)
     second_part = back_dot(dglin, w_gate) + back_dot(dulin, w_up)
-    dnormed2 = lax.psum(second_part, "tensor")
+    dnormed2 = jnp.sum(lax.all_gather(second_part, "tensor"), axis=0)
     grad_ffn_gain = jnp.sum(dnormed2 * unit_second, axis=0)
     dresid = cotangent.astype(jnp.float32) + rms_back(dnormed2, unit_second, inv_second, ffn_gain)
     dresid_bf = dresid.astype(jnp.bfloat16)

time: 1250 us -> 1160 us (0.928)
  waiting for transfers between devices: 767 us -> 731 us
  other arithmetic: 80.2 us -> 52.9 us
  local copies, waits for them, and re-layouts: 107 us -> 82.2 us
  matrix products: 230 us -> 210 us
    reduce_scatter x1, waiting for transfers between devices: 75.8 us -> 34 us  [local(): lax.psum_scatter(grad_gate, 'dp', scatter_dimension=0, tiled=True)]
    psum x1 -> x0, waiting for transfers between devices: 36 us -> none  [local(): dnormed2 = lax.psum(second_part, 'tensor')]
    all_gather x0 -> x1, waiting for transfers between devices: none -> 32.5 us  [local(): dnormed2 = jnp.sum(lax.all_gather(second_part, 'tensor'), axis=0)]
    reduce_scatter x1, waiting for transfers between devices: 52.1 us -> 67.3 us  [local(): lax.psum_scatter(grad_key, 'dp', scatter_dimension=0, tiled=True)]
  transfers between devices with their start and end apart: 14 -> 14, of which waited for: 13 -> 13; matrix products, arithmetic and copies ran while one was open for 3% -> 17% of each run, Pallas kernels for 0% -> 0%
where the time goes in v1:
time: 1160 us; the launch traced here: 1150 us
  waiting for transfers between devices  731 us (63%)
  matrix products  210 us (18%)
  local copies, waits for them, and re-layouts  82.2 us (7%)
  other arithmetic  52.9 us (5%)
  blocking collectives  45 us (4%)
  between operations  16.3 us (1%)
    unnamed x16, waiting for transfers between devices  97.5 us
    reduce_scatter x1, waiting for transfers between devices, local(): lax.psum_scatter(grad_up, 'dp', scatter_dimension=0, tiled=True)  76.2 us
    reduce_scatter x1, waiting for transfers between devices, local(): lax.psum_scatter(grad_down, 'dp', scatter_dimension=0, tiled=True)  76.2 us
    reduce_scatter x1, waiting for transfers between devices, local(): lax.psum_scatter(grad_out, 'dp', scatter_dimension=0, tiled=True)  71.5 us
    reduce_scatter x1, waiting for transfers between devices, local(): lax.psum_scatter(grad_value, 'dp', scatter_dimension=0, tiled=True)  71.5 us
    reduce_scatter x1, waiting for transfers between devices, local(): lax.psum_scatter(grad_outgate, 'dp', scatter_dimension=0, tiled=True)  71.4 us
    reduce_scatter x1, waiting for transfers between devices, local(): lax.psum_scatter(grad_query, 'dp', scatter_dimension=0, tiled=True)  67.3 us
    reduce_scatter x1, waiting for transfers between devices, local(): lax.psum_scatter(grad_key, 'dp', scatter_dimension=0, tiled=True)  67.3 us
  transfers between devices with their start and end apart: 14, of which 13 were waited for; matrix products, arithmetic and copies ran while one was open for 17% of the time, Pallas kernels for 0%

profile of v1, /device:TPU:0, one launch (start us, length us, event | category | flops | bytes accessed | tf_op | source)
XLA Modules:
  0.0 1149.2 jit_solution(3605929312712483802)
XLA Ops:
  7.3 1.3 fusion.260
  9.5 1.6 fusion.306
  20.3 1.7 fusion.305
  28.9 103.5 %while.116 = (s32[]{:T(128)}, f32[2,256,128]{2,1,0:T(8,128)S(1)}, f32[4,64,2,256]{3,1,2,0:T(8,128)}, f32[4,64,64,2]{1,2,3,0:T(8,128)}, f32[4,64,2]{1,2,0:T(2,128...) while((s32[]{:T(128)}, f32[2,256,128]{2,1,0:T(8,128)S(1)}, ...), condition=%wide.region_5.6_spmd.clone.clone, body=%wide.region_3.5_spmd.clone.clone.sunk | while | flops 290349312 | bytes 8164578 | solution.py:72
  41.5 1.8 bitcast_dynamic-update-slice_fusion.53
  43.3 1.7 bitcast_dynamic-update-slice_fusion.54
  46.9 1.8 fusion.542
  67.3 1.8 bitcast_dynamic-update-slice_fusion.53
  69.2 1.7 bitcast_dynamic-update-slice_fusion.54
  72.8 1.7 fusion.542
  93.3 1.8 bitcast_dynamic-update-slice_fusion.53
  95.1 1.7 bitcast_dynamic-update-slice_fusion.54
  98.8 1.7 fusion.542
  119.2 1.8 bitcast_dynamic-update-slice_fusion.53
  121.0 1.6 bitcast_dynamic-update-slice_fusion.54
  124.6 1.7 fusion.542
  132.3 1.3 multiply_reduce_fusion.11
  133.6 1.4 copy.477
  136.5 1.3 multiply_convert_fusion.5
  138.5 1.4 fusion.319
  140.0 9.8 all-gather.3.cloned.1.call-start
  149.8 29.3 %all-reduce.33.cloned.1.call-done = f32[256,1024]{1,0:T(8,128)} async-done(((f32[256,1024]{1,0:T(8,128)}), f32[256,1024]{1,0:T(8,128)}) %all-reduce.33.cloned.1.call-update) | async-done | bytes 1048592 | tf_op jit(solution)/shard_map/psum | solution.py:152
  179.1 1.4 multiply_reduce_fusion.4
  180.8 1.5 copy-done.11
  186.5 1.6 convolution_add_fusion.18
  189.0 1.6 fusion.322
  190.7 32.5 %all-gather.3.cloned.1.call-done = f32[1024,1024]{1,0:T(8,128)} async-done(((f32[256,1024]{1,0:T(8,128)}), f32[1024,1024]{1,0:T(8,128)}) %all-gather.3.cloned.1.call-update) | async-done | bytes 4194320 | tf_op jit(solution)/shard_map/all_gather | solution.py:173
  223.2 2.8 reduce_sum.527
  229.1 1.3 fusion.286
  231.7 1.4 add_add_fusion
  236.1 144.3 %while.117 = (s32[]{:T(128)}, f32[2,256,128]{2,1,0:T(8,128)S(1)}, f32[4,64,2,128]{3,1,2,0:T(8,128)}, f32[4,64,2,128]{3,1,2,0:T(8,128)}, f32[4,64,2,256]{3,2,1,0:...) while((s32[]{:T(128)}, f32[2,256,128]{2,1,0:T(8,128)S(1)}, ...), condition=%wide.region_24.25_spmd.clone.clone, body=%wide.region_13.24_spmd.clone.clone.sunk | while | flops 580338304 | bytes 14117188 | solution.py:72
  236.2 1.3 fusion.607
  272.2 1.3 fusion.607
  308.2 1.3 fusion.607
  344.3 1.3 fusion.607
  370.2 1.3 fusion.626
  393.9 1.4 fusion.324
  399.7 1.4 convolution_add_fusion.15
  401.2 2.1 fusion.327
  404.2 2.2 fusion.328
  407.5 2.2 convolution_bitcast_fusion.7
  409.8 1.4 fusion.301
  411.3 1.4 fusion.302
  412.8 1.8 fusion.280
  414.7 1.9 fusion.300
  416.6 2.0 fusion.299
  418.8 1.8 dynamic-slice_add_fusion.1
  420.6 6.3 psum.85
  427.0 33.9 %reduce-scatter.34.cloned.1.call-done = f32[128,2]{1,0:T(8,128)} async-done(((f32[1024,2]{1,0:T(8,128)}), f32[128,2]{1,0:T(8,128)}) %reduce-scatter.34.cloned.1.call-update) | async-done | bytes 1040
  460.9 1.5 copy.540
  462.4 63.4 %reduce-scatter.36.cloned.1.call-done = f32[128,2]{1,0:T(8,128)} async-done(((f32[1024,2]{1,0:T(8,128)}), f32[128,2]{1,0:T(8,128)}) %reduce-scatter.36.cloned.1.call-update) | async-done | bytes 1040
  525.8 1.5 copy.542
  527.3 36.1 %all-reduce.35.cloned.1.call-done = f32[256,1024]{1,0:T(8,128)} async-done(((f32[256,1024]{1,0:T(8,128)}), f32[256,1024]{1,0:T(8,128)}) %all-reduce.35.cloned.1.call-update) | async-done | bytes 1048592 | tf_op jit(solution)/shard_map/psum | solution.py:203
  563.3 3.0 multiply_reduce_fusion.1
  566.3 38.7 %all-reduce.29 = (f32[1024]{0:T(1024)}, f32[4,256]{1,0:T(4,128)}, f32[4,256]{1,0:T(4,128)}, f32[4,512]{1,0:T(4,128)}, f32[2]{0:T(128)}, /*index=5*/f32[2]{0:T(128)}, f32[256]{0:T(256)}, f32[1024]{0:T(1024)}) all-reduce(f32[1024]{0:T(1024)S(1)} %get-tuple-element.2794, ...), channel_id=1, replica_groups=mesh['dp'=8,'tensor'=4] {'dp'}, use_global_device_ids=true, to_apply=%region_30.31 | all-reduce | flops 6404 | bytes 51232 | tf_op jit(solution)/shard_map/psum | solution.py:208
  605.1 1.9 dynamic-slice_add_fusion
  606.9 34.0 %reduce-scatter.28.cloned.1.call-done = f32[128,704]{0,1:T(8,128)} async-done(((f32[1024,704]{0,1:T(8,128)}), f32[128,704]{0,1:T(8,128)}) %reduce-scatter.28.cloned.1.call-update) | async-done | bytes 360464 | tf_op jit(solution)/shard_map/reduce_scatter | solution.py:241
  641.0 76.2 %reduce-scatter.30.cloned.1.call-done = f32[128,704]{0,1:T(8,128)} async-done(((f32[1024,704]{0,1:T(8,128)}), f32[128,704]{0,1:T(8,128)}) %reduce-scatter.30.cloned.1.call-update) | async-done | bytes 360464 | tf_op jit(solution)/shard_map/reduce_scatter | solution.py:242
  717.2 76.2 %reduce-scatter.32.cloned.1.call-done = f32[128,704]{0,1:T(8,128)} async-done(((f32[1024,704]{0,1:T(8,128)}), f32[128,704]{0,1:T(8,128)}) %reduce-scatter.32.cloned.1.call-update) | async-done | bytes 360464 | tf_op jit(solution)/shard_map/reduce_scatter | solution.py:243
  793.3 67.3 %reduce-scatter.20.cloned.1.call-done = f32[128,256]{1,0:T(8,128)} async-done(((f32[1024,256]{1,0:T(8,128)}), f32[128,256]{1,0:T(8,128)}) %reduce-scatter.20.cloned.1.call-update) | async-done | bytes 131088 | tf_op jit(solution)/shard_map/reduce_scatter | solution.py:235
  860.6 67.3 %reduce-scatter.18.cloned.1.call-done = f32[128,256]{1,0:T(8,128)} async-done(((f32[1024,256]{1,0:T(8,128)}), f32[128,256]{1,0:T(8,128)}) %reduce-scatter.18.cloned.1.call-update) | async-done | bytes 131088 | tf_op jit(solution)/shard_map/reduce_scatter | solution.py:234
  927.9 71.5 %reduce-scatter.26.cloned.1.call-done = f32[128,512]{1,0:T(8,128)} async-done(((f32[1024,512]{1,0:T(8,128)}), f32[128,512]{1,0:T(8,128)}) %reduce-scatter.26.cloned.1.call-update) | async-done | bytes 262160 | tf_op jit(solution)/shard_map/reduce_scatter | solution.py:240
  999.4 71.5 %reduce-scatter.22.cloned.1.call-done = f32[128,512]{1,0:T(8,128)} async-done(((f32[1024,512]{1,0:T(8,128)}), f32[128,512]{1,0:T(8,128)}) %reduce-scatter.22.cloned.1.call-update) | async-done | bytes 262160 | tf_op jit(solution)/shard_map/reduce_scatter | solution.py:236
  1070.9 71.4 %reduce-scatter.24.cloned.1.call-done = f32[128,512]{1,0:T(8,128)} async-done(((f32[1024,512]{1,0:T(8,128)}), f32[128,512]{1,0:T(8,128)}) %reduce-scatter.24.cloned.1.call-update) | async-done | bytes 262160 | tf_op jit(solution)/shard_map/reduce_scatter | solution.py:237
  (899 shorter events, 269.4 us)
Async XLA Ops:
  7.2 177.3 %copy-start = (bf16[1024,704]{0,1:T(8,128)(2,1)S(1)}, bf16[1024,704]{0,1:T(8,128)(2,1)}, u32[]{:S(2)}) copy-start(bf16[1024,704]{0,1:T(8,128)(2,1)} %param.42) | copy-start | bytes 4325380
  7.2 171.9 %all-reduce.33.cloned.1.call-start = ((), (), s32[]{:S(2)}) async-start(), calls=%async_computation.11 | async-start | bytes 2097152 | tf_op jit(solution)/shard_map/psum | solution.py:152
  8.6 18.1 %copy-start.73 = (f32[256]{0:T(256)}, f32[256]{0:T(256)S(1)}, u32[]{:S(2)}) copy-start(f32[256]{0:T(256)S(1)} %add_rsqrt_fusion.3) | copy-start | bytes 3076
  14.6 5.7 copy-start.16
  15.6 12.2 %copy-start.64 = (pred[64,64]{1,0:T(8,128)(4,1)}, pred[64,64]{1,0:T(8,128)(4,1)S(1)}, u32[]{:S(2)}) copy-start(pred[64,64]{1,0:T(8,128)(4,1)S(1)} %get-tuple-element.3993) | copy-start | bytes 12292
  30.8 8.3 copy-start.28
  45.0 5.2 copy-start.29
  45.0 5.2 copy-start.41
  56.6 8.2 copy-start.28
  70.9 5.2 copy-start.29
  70.9 5.2 copy-start.41
  82.5 8.3 copy-start.28
  96.8 5.2 copy-start.29
  96.8 5.2 copy-start.41
  108.5 8.3 copy-start.28
  122.7 5.2 copy-start.29
  122.7 5.2 copy-start.41
  135.1 95.7 %copy-start.76 = (f32[4,64,2]{1,2,0:T(2,128)}, f32[4,64,2]{1,2,0:T(2,128)S(1)}, u32[]{:S(2)}) copy-start(f32[4,64,2]{1,2,0:T(2,128)S(1)} %fusion.287) | copy-start | bytes 6148
  140.0 40.6 %copy-start.79 = (f32[1024]{0:T(1024)S(1)}, f32[1024]{0:T(1024)}, u32[]{:S(2)}) copy-start(f32[1024]{0:T(1024)} %param.39) | copy-start | bytes 12292
  140.0 83.2 %all-gather.3.cloned.1.call-start = ((), (), s32[]{:S(2)}) async-start(), calls=%async_computation.22 | async-start | bytes 5242880 | tf_op jit(solution)/shard_map/all_gather | solution.py:173
  188.1 230.6 %reduce-scatter.16.cloned.1.call-start = ((), (), s32[]{:S(2)}) async-start(), calls=%async_computation.12 | async-start | bytes 1310720 | tf_op jit(solution)/shard_map/reduce_scatter | solution.py:164
  190.6 270.3 %reduce-scatter.34.cloned.1.call-start = ((), (), s32[]{:S(2)}) async-start(), calls=%async_computation.23 | async-start | bytes 589824
  236.2 7.6 copy-start.32
  236.2 4.8 copy-start.33
  237.5 9.0 copy-start.31
  243.7 9.8 copy-start.30
  256.9 6.5 copy-start.80
  272.1 7.6 copy-start.32
  273.4 9.0 copy-start.31
  279.7 9.8 copy-start.30
  292.8 6.6 copy-start.80
  308.2 7.6 copy-start.32
  309.5 9.0 copy-start.31
  315.8 9.8 copy-start.30
  328.9 6.6 copy-start.80
  344.3 7.6 copy-start.32
  344.3 4.8 copy-start.33
  345.6 9.0 copy-start.31
  351.8 9.8 copy-start.30
  365.0 6.5 copy-start.80
  398.1 127.7 %reduce-scatter.36.cloned.1.call-start = ((), (), s32[]{:S(2)}) async-start(), calls=%async_computation.24 | async-start | bytes 589824
  399.7 163.7 %all-reduce.35.cloned.1.call-start = ((), (), s32[]{:S(2)}) async-start(), calls=%async_computation.13 | async-start | bytes 2097152 | tf_op jit(solution)/shard_map/psum | solution.py:203
  401.1 239.8 %reduce-scatter.28.cloned.1.call-start = ((), (), s32[]{:S(2)}) async-start(), calls=%async_computation.19 | async-start | bytes 3244032 | tf_op jit(solution)/shard_map/reduce_scatter | solution.py:241
  403.3 313.9 %reduce-scatter.30.cloned.1.call-start = ((), (), s32[]{:S(2)}) async-start(), calls=%async_computation.20 | async-start | bytes 3244032 | tf_op jit(solution)/shard_map/reduce_scatter | solution.py:242
  406.4 386.9 %reduce-scatter.32.cloned.1.call-start = ((), (), s32[]{:S(2)}) async-start(), calls=%async_computation.21 | async-start | bytes 3244032 | tf_op jit(solution)/shard_map/reduce_scatter | solution.py:243
  409.7 450.8 %reduce-scatter.20.cloned.1.call-start = ((), (), s32[]{:S(2)}) async-start(), calls=%async_computation.15 | async-start | bytes 1179648 | tf_op jit(solution)/shard_map/reduce_scatter | solution.py:235
  411.3 516.6 %reduce-scatter.18.cloned.1.call-start = ((), (), s32[]{:S(2)}) async-start(), calls=%async_computation.14 | async-start | bytes 1179648 | tf_op jit(solution)/shard_map/reduce_scatter | solution.py:234
  412.8 586.6 %reduce-scatter.26.cloned.1.call-start = ((), (), s32[]{:S(2)}) async-start(), calls=%async_computation.18 | async-start | bytes 2359296 | tf_op jit(solution)/shard_map/reduce_scatter | solution.py:240
  414.7 656.2 %reduce-scatter.22.cloned.1.call-start = ((), (), s32[]{:S(2)}) async-start(), calls=%async_computation.16 | async-start | bytes 2359296 | tf_op jit(solution)/shard_map/reduce_scatter | solution.py:236
  416.6 725.7 %reduce-scatter.24.cloned.1.call-start = ((), (), s32[]{:S(2)}) async-start(), calls=%async_computation.17 | async-start | bytes 2359296 | tf_op jit(solution)/shard_map/reduce_scatter | solution.py:237
  418.6 8.3 copy-start.126
  418.6 8.3 copy-start.127
  418.6 8.3 copy-start.128
  418.6 8.3 copy-start.129
  418.6 8.3 copy-start.130
  418.6 8.3 copy-start.131
  418.7 8.3 copy-start.132
  418.7 8.3 copy-start.133
  418.7 8.3 copy-start.120
  418.7 8.3 copy-start.121
  418.7 8.3 copy-start.143
  527.3 39.1 %copy-start.98 = (f32[1024]{0:T(1024)S(1)}, f32[1024]{0:T(1024)}, u32[]{:S(2)}) copy-start(f32[1024]{0:T(1024)} %get-tuple-element.2786) | copy-start | bytes 12292
  527.3 39.1 %copy-start.138 = (f32[2]{0:T(128)S(1)}, f32[2]{0:T(128)}, u32[]{:S(2)}) copy-start(f32[2]{0:T(128)} %get-tuple-element.2998) | copy-start | bytes 28
  563.3 579.0 %copy-start.1 = (bf16[1024,704]{0,1:T(8,128)(2,1)S(1)}, bf16[1024,704]{0,1:T(8,128)(2,1)}, u32[]{:S(2)}) copy-start(bf16[1024,704]{0,1:T(8,128)(2,1)} %param.42) | copy-start | bytes 4325380
  (128 other events, 250.7 us)
Sparse Core Ops, SparseCore 0:
  140.1 38.9 all-reduce.32
  188.3 34.9 all-gather.2
  225.8 24.7 reduce-scatter.15
  398.2 62.6 reduce-scatter.33
  464.1 61.6 reduce-scatter.35
  528.0 35.2 all-reduce.34
  567.4 73.4 reduce-scatter.27
  645.1 72.0 reduce-scatter.29
  721.3 71.9 reduce-scatter.31
  797.1 63.3 reduce-scatter.19
  864.6 63.2 reduce-scatter.17
  931.8 67.5 reduce-scatter.25
  1003.5 67.3 reduce-scatter.21
  1074.8 67.4 reduce-scatter.23
